TPU v7x, 32 devices: a whole 2x2x4 slice. The times are simulated.
32 devices in a mesh: tiles: 8 (over z, x), lev: 4 (over y, core).
Axes of the slice: x: 2, y: 2, z: 4, core: 2. Of those that a mesh axis runs over, the one named last changes fastest.
Arguments:
- land_smb: bfloat16 [512, 10, 128], P(('tiles', 'lev')), may hold values from -6 to 6
- block_weights: bfloat16 [1024, 128, 1024], P(('tiles', 'lev')), may hold values from -0.5 to 0.5
- block_tile: int32 [1024], P(('tiles', 'lev')), may hold values from 0 to 255, as said below
- block_land: int32 [1024], P(('tiles', 'lev')), may hold values from 0 to 15
- block_class: int32 [1024], P(('tiles', 'lev')), may hold values from 0 to 9
- ice_mask: int32 [64, 4096], P('tiles', 'lev'), may hold values 0 or 1
- thickness: float32 [64, 4096], P('tiles', 'lev'), may hold values from 0.5 to 2
- prev_smb: float32 [64, 4096], P('tiles', 'lev'), may hold values from -6 to 6
- basal_friction: float32 [64, 4096], P('tiles', 'lev'), may hold values from 0.05 to 0.5
- driving: float32 [10, 64, 4096], P(None, 'tiles', 'lev'), may hold values from -54 to 54
- velocity_start: float32 [10, 64, 4096], P(None, 'tiles', 'lev'), may hold values from -6 to 6
Outputs:
- ice_smb: float32 [64, 4096], P('tiles')
- velocity_end: float32 [10, 64, 4096], P(None, 'tiles', 'lev')
Inputs may be any that keep to these rules, and one draw needn't show every extreme that they name: `block_tile`: ice tile t lies on index t // 32 of tiles. Of the 32 remap blocks of one device, at most 8 name tiles on any one index of tiles; in every draw some index of tiles receives exactly 8 from every device.
All inputs are finite; a program needn't handle non-finite values. No bound on the sum of `ice_mask` on one device may be relied on, other than what follows from the above.
Results may differ from a plain program's by a relative error of at most 0.0003.
Values sent between devices are 32-bit elements; how exact they have to be, the bound alone decides.
A program may use at most 64 MiB of HBM per device.

v0:
```python
import jax
import jax.numpy as jnp
from jax import lax
from jax.sharding import PartitionSpec as P

CX = 8
TW = 128
TPD = 32
ITERS = 4


VISC_FLOOR = 0.25
VERTICAL = 4.0
SMB_WEIGHT = 0.5


def extended(cells, sides, width):
    for axis, dim in sides:
        count = lax.axis_size(axis)
        ends = count - 1
        head = lax.slice_in_dim(cells, 0, width, axis=dim)
        tail = lax.slice_in_dim(cells, cells.shape[dim] - width, cells.shape[dim], axis=dim)
        cells = jnp.concatenate(
            [
                lax.ppermute(tail, axis, [(i, (i + 1) % count) for i in range(ends)]),
                cells,
                lax.ppermute(head, axis, [((i + 1) % count, i) for i in range(ends)]),
            ],
            axis=dim,
        )
    return cells


def visc_from(box, ice_frac):
    slope_x = (box[:, 2:, 1:-1] - box[:, :-2, 1:-1]) * 0.5
    slope_y = (box[:, 1:-1, 2:] - box[:, 1:-1, :-2]) * 0.5
    return ice_frac * (VISC_FLOOR + slope_x * slope_x + slope_y * slope_y) ** (-1.0 / 3.0)


def level_pad(box):
    return jnp.pad(box, ((1, 1), (0, 0), (0, 0)))


def face_weights(visc_box, drag):
    center = visc_box[1:-1, 1:-1, 1:-1]
    east_face = jnp.sqrt(center * visc_box[1:-1, 2:, 1:-1])
    west_face = jnp.sqrt(center * visc_box[1:-1, :-2, 1:-1])
    north_face = jnp.sqrt(center * visc_box[1:-1, 1:-1, 2:])
    south_face = jnp.sqrt(center * visc_box[1:-1, 1:-1, :-2])
    upper_face = VERTICAL * jnp.sqrt(center * visc_box[2:, 1:-1, 1:-1])
    lower_face = VERTICAL * jnp.sqrt(center * visc_box[:-2, 1:-1, 1:-1])
    diagonal_sum = drag + east_face + west_face + north_face + south_face + upper_face + lower_face
    return (diagonal_sum, east_face, west_face, upper_face, lower_face, north_face, south_face)


def apply_operator(faces, field_box):
    diagonal_sum, east_face, west_face, upper_face, lower_face, north_face, south_face = faces
    center = field_box[1:-1, 1:-1, 1:-1]
    result = (
        diagonal_sum * center
        - east_face * field_box[1:-1, 2:, 1:-1]
        - west_face * field_box[1:-1, :-2, 1:-1]
    )
    result = (
        result - upper_face * field_box[2:, 1:-1, 1:-1] - lower_face * field_box[:-2, 1:-1, 1:-1]
    )
    return result - north_face * field_box[1:-1, 1:-1, 2:] - south_face * field_box[1:-1, 1:-1, :-2]


def apply_local(faces, field):
    field_box = extended(field, (("tiles", 1), ("lev", 2)), 1)
    return apply_operator(faces, level_pad(field_box))


def paired_totals(residual, image):
    return lax.psum((jnp.sum(residual * residual), jnp.sum(residual * image)), ("tiles", "lev"))


def krylov_merged(faces, rhs, start):
    solution = start
    residual = rhs - apply_local(faces, start)
    image = apply_local(faces, residual)
    norm_now, product = paired_totals(residual, image)
    step_len = norm_now / product
    direction = residual
    along = image
    for iteration in range(ITERS):
        solution = solution + step_len * direction
        residual = residual - step_len * along
        if iteration + 1 < ITERS:
            image = apply_local(faces, residual)
            norm_next, product = paired_totals(residual, image)
            ratio = norm_next / norm_now
            step_len = norm_next / (product - ratio * norm_next / step_len)
            direction = residual + ratio * direction
            along = image + ratio * along
            norm_now = norm_next
    return solution


def sent_visc(velocity, ice_frac):
    x_box = extended(velocity, (("tiles", 1), ("lev", 2)), 1)
    viscosity = visc_from(x_box, ice_frac)
    visc_box = extended(viscosity, (("tiles", 1), ("lev", 2)), 1)
    return level_pad(visc_box)


def body(
    land_smb,
    block_weights,
    block_tile,
    block_land,
    block_class,
    ice_mask,
    thickness,
    prev_smb,
    basal_friction,
    driving,
    velocity_start,
):
    local_blocks, classes, land_cols = land_smb.shape
    blocks_here = block_tile.shape[0]
    tile_cells = block_weights.shape[2]
    land_rows = land_smb.reshape(local_blocks * classes, land_cols)
    picked = land_rows[block_land * classes + block_class]
    products = jnp.einsum("bl,blt->bt", picked, block_weights, preferred_element_type=jnp.float32)
    owners = lax.axis_size("tiles")
    capacity = max(2, 2 * blocks_here // owners)
    destination = block_tile // TPD
    local_tile = block_tile % TPD
    positions = jnp.arange(blocks_here, dtype=jnp.int32)
    earlier = jnp.logical_and(
        destination[None, :] == destination[:, None], positions[None, :] < positions[:, None]
    )
    ranks = jnp.sum(earlier.astype(jnp.int32), axis=1)
    slots = destination * capacity + ranks
    slot_ids = jnp.arange(owners * capacity, dtype=jnp.int32)
    slot_match = slots[None, :] == slot_ids[:, None]
    slot_hot = slot_match.astype(jnp.float32)
    sending = jnp.dot(
        slot_hot, products, precision=lax.Precision.HIGHEST, preferred_element_type=jnp.float32
    )
    sending = sending.reshape(owners, capacity, tile_cells)
    slot_tile = jnp.sum(jnp.where(slot_match, (local_tile + 1)[None, :], 0), axis=1) - 1
    slot_tile = slot_tile.reshape(owners, capacity)
    received, recv_tile = (
        lax.all_to_all(sending, "tiles", split_axis=0, concat_axis=0, tiled=True),
        lax.all_to_all(slot_tile, "tiles", split_axis=0, concat_axis=0, tiled=True),
    )
    tile_hot = (recv_tile.reshape(-1)[None, :] == jnp.arange(TPD, dtype=jnp.int32)[:, None]).astype(
        jnp.float32
    )
    partial_sums = jnp.dot(
        tile_hot,
        received.reshape(-1, tile_cells),
        precision=lax.Precision.HIGHEST,
        preferred_element_type=jnp.float32,
    )
    totals = lax.psum(partial_sums, "lev")
    ice_smb = totals.reshape(TPD, CX, TW).transpose(1, 0, 2).reshape(CX, TPD * TW)
    ice_frac = ice_mask.astype(jnp.float32)
    rhs = (ice_frac * (thickness + SMB_WEIGHT * prev_smb))[None] * driving
    drag = (ice_frac * basal_friction + (1.0 - ice_frac))[None]
    velocity = velocity_start
    visc_box = sent_visc(velocity, ice_frac[None])
    faces = face_weights(visc_box, drag)
    velocity = krylov_merged(faces, rhs, velocity)
    return (ice_smb, velocity)


def solution(mesh):
    in_specs = (
        P(("tiles", "lev"), None, None),
        P(("tiles", "lev"), None, None),
        P(("tiles", "lev")),
        P(("tiles", "lev")),
        P(("tiles", "lev")),
        P("tiles", "lev"),
        P("tiles", "lev"),
        P("tiles", "lev"),
        P("tiles", "lev"),
        P(None, "tiles", "lev"),
        P(None, "tiles", "lev"),
    )
    out_specs = (P("tiles", None), P(None, "tiles", "lev"))
    return jax.shard_map(body, mesh=mesh, in_specs=in_specs, out_specs=out_specs, check_vma=False)
```

profile of v0, /device:TPU:0, one launch (start us, length us, event | category | flops | bytes accessed | tf_op | source)
XLA Modules:
  0.0 379.7 jit_solution(6685467221838924000)
XLA Ops:
  7.2 1.1 fusion.96
  8.3 1.3 collective-permute-start
  9.6 5.5 %collective-permute-start.1 = (f32[10,1,1024]{2,1,0:T(1,128)S(1)}, f32[10,1,1024]{2,1,0:T(1,128)S(1)}, u32[]{:S(2)}, u32[]{:S(2)}) collective-permute-start(f32[10,1,1024]{2,1,0:T(1,128)S(1)} %get-tuple-element.46), channel_id=1, source_target_pairs={{0,4},{4,8},{8,12},{12,16},{16,20},{20,24},{24,28},{1,5},{5,9},{9,... | collective-permute-start | bytes 122888 | tf_op jit(solution)/shard_map/ppermute | solution.py:25
  15.2 1.6 collective-permute-done.1
  16.8 1.1 pad_maximum_fusion
  18.0 1.3 collective-permute-start.2
  19.3 3.0 collective-permute-start.3
  22.3 1.4 add_multiply_fusion
  23.7 0.8 convert_element_type.16
  24.5 2.2 power_multiply_fusion
  26.8 1.3 collective-permute-start.4
  28.1 5.4 %collective-permute-start.5 = (f32[10,1,1024]{2,1,0:T(1,128)S(1)}, f32[10,1,1024]{2,1,0:T(1,128)S(1)}, u32[]{:S(2)}, u32[]{:S(2)}) collective-permute-start(f32[10,1,1024]{2,1,0:T(1,128)S(1)} %get-tuple-element.44), channel_id=1, source_target_pairs={{0,4},{4,8},{8,12},{12,16},{16,20},{20,24},{24,28},{1,5},{5,9},{9,... | collective-permute-start | bytes 122888 | tf_op jit(solution)/shard_map/ppermute | solution.py:25
  33.5 1.2 fusion.79
  34.7 0.9 collective-permute-done.5
  35.9 1.3 collective-permute-start.6
  37.2 3.0 collective-permute-start.7
  42.0 3.4 fusion.11
  45.5 1.3 collective-permute-start.8
  46.8 5.4 %collective-permute-start.9 = (f32[10,1,1024]{2,1,0:T(1,128)S(1)}, f32[10,1,1024]{2,1,0:T(1,128)S(1)}, u32[]{:S(2)}, u32[]{:S(2)}) collective-permute-start(f32[10,1,1024]{2,1,0:T(1,128)S(1)} %get-tuple-element.42), channel_id=1, source_target_pairs={{0,4},{4,8},{8,12},{12,16},{16,20},{20,24},{24,28},{1,5},{5,9},{9,... | collective-permute-start | bytes 122888 | tf_op jit(solution)/shard_map/ppermute | solution.py:25
  52.9 1.0 collective-permute-done.9
  54.1 3.5 collective-permute-start.10
  57.6 1.3 collective-permute-start.11
  59.6 3.9 %collective-permute-done.11 = f32[10,10,1]{2,1,0:T(8,128)S(1)} collective-permute-done((f32[10,10,1]{2,1,0:T(8,128)S(1)}, f32[10,10,1]{2,1,0:T(8,128)S(1)}, u32[]{:S(2)}, u32[]{:S(2)}) %collective-permute-start.11) | collective-permute-done | bytes 432 | tf_op jit(solution)/shard_map/ppermute | solution.py:27
  63.5 1.1 concatenate.129
  64.6 3.3 multiply_reduce_fusion.5
  67.9 45.4 %all-reduce.9 = (f32[]{:T(128)}, f32[]{:T(128)}) all-reduce(f32[]{:T(128)} %get-tuple-element.7, f32[]{:T(128)} %get-tuple-element.6), channel_id=1, replica_groups=mesh['tiles'=8,'lev'=4] {'tiles','lev'}, use_global_device_ids=true, to_apply=%region_4.5 | all-reduce | flops 2 | bytes 16 | tf_op jit(solution)/shard_map/psum | solution.py:76
  114.6 1.3 collective-permute-start.12
  115.9 4.8 %collective-permute-start.13 = (f32[10,1,1024]{2,1,0:T(1,128)S(1)}, f32[10,1,1024]{2,1,0:T(1,128)S(1)}, u32[]{:S(2)}, u32[]{:S(2)}) collective-permute-start(f32[10,1,1024]{2,1,0:T(1,128)S(1)} %get-tuple-element.40), channel_id=1, source_target_pairs={{0,4},{4,8},{8,12},{12,16},{16,20},{20,24},{24,28},{1,5},{5,9},{9,... | collective-permute-start | bytes 122888 | tf_op jit(solution)/shard_map/ppermute | solution.py:25
  121.4 5.9 %all-to-all-start = ((s32[8,1,8]{2,1,0:T(1,128)}), s32[8,1,8]{2,1,0:T(1,128)}, u32[]{:S(2)}, u32[]{:S(2)}) async-start(s32[8,1,8]{2,1,0:T(1,128)} %bitcast), calls=%async_computation | async-start | bytes 8192 | tf_op jit(solution)/shard_map/all_to_all | solution.py:148
  127.6 1.3 collective-permute-start.14
  128.9 1.3 collective-permute-start.15
  130.2 1.2 compare_select_fusion
  131.4 3.0 collective-permute-done.15
  134.4 1.1 concatenate.135
  135.6 3.3 multiply_reduce_fusion.3
  138.8 42.6 %all-reduce.8 = (f32[]{:T(128)}, f32[]{:T(128)}) all-reduce(f32[]{:T(128)} %get-tuple-element.5, f32[]{:T(128)} %get-tuple-element.4), channel_id=1, replica_groups=mesh['tiles'=8,'lev'=4] {'tiles','lev'}, use_global_device_ids=true, to_apply=%region_8.9 | all-reduce | flops 2 | bytes 16 | tf_op jit(solution)/shard_map/psum | solution.py:76
  186.2 1.3 collective-permute-start.16
  187.5 4.8 %collective-permute-start.17 = (f32[10,1,1024]{2,1,0:T(1,128)S(1)}, f32[10,1,1024]{2,1,0:T(1,128)S(1)}, u32[]{:S(2)}, u32[]{:S(2)}) collective-permute-start(f32[10,1,1024]{2,1,0:T(1,128)S(1)} %get-tuple-element.38), channel_id=1, source_target_pairs={{0,4},{4,8},{8,12},{12,16},{16,20},{20,24},{24,28},{1,5},{5,9},{9,... | collective-permute-start | bytes 122888 | tf_op jit(solution)/shard_map/ppermute | solution.py:25
  193.0 0.8 copy.18
  194.5 1.0 pad_maximum_fusion.4
  195.4 1.0 fusion.86
  196.5 1.3 collective-permute-start.18
  197.8 1.5 collective-permute-start.19
  199.2 5.2 %fusion.74 = f32[32,1,1024]{2,1,0:T(1,128)} fusion(bf16[32,128,1024]{2,1,0:T(8,128)(2,1)} %param.12, bf16[32,128,1]{1,0,2:T(8,128)(2,1)S(1)} %bitcast.19), kind=kOutput, calls=%fused_computation.159 | convolution fusion | flops 8388608 | bytes 8527872 | tf_op jit(solution)/shard_map/bl,blt->bt/dot_general | solution.py:126
  204.5 2.3 concatenate.141
  206.8 4.0 %multiply_reduce_fusion.1 = (f32[]{:T(128)}, f32[]{:T(128)}, f32[10,8,1024]{2,1,0:T(8,128)}) fusion(f32[10,8,1024]{2,1,0:T(8,128)S(1)} %multiply_subtract_fusion.1, f32[10,1,1024]{2,1,0:T(1,128)S(1)} %collective-permute-done.16, f32[10,1,1024]{2,1,0:T(1,128)S(1)} %collective-permute-done.17, f32[10,10,1]{2,1,0:T(8,128)S(1)} %collective-permute-done.18, ...), kind=kLoop, calls=%fused_computation.142 | loop fusion | flops 3522558 | bytes 2247016 | tf_op jit(solution)/shard_map/reduce_sum | solution.py:76
  210.8 44.5 %all-reduce.7 = (f32[]{:T(128)}, f32[]{:T(128)}) all-reduce(f32[]{:T(128)} %get-tuple-element.3, f32[]{:T(128)} %get-tuple-element.2), channel_id=1, replica_groups=mesh['tiles'=8,'lev'=4] {'tiles','lev'}, use_global_device_ids=true, to_apply=%region_12.13 | all-reduce | flops 2 | bytes 16 | tf_op jit(solution)/shard_map/psum | solution.py:76
  259.1 1.8 multiply_reduce_fusion
  260.9 1.3 collective-permute-start.20
  262.2 4.8 %collective-permute-start.21 = (f32[10,1,1024]{2,1,0:T(1,128)S(1)}, f32[10,1,1024]{2,1,0:T(1,128)S(1)}, u32[]{:S(2)}, u32[]{:S(2)}) collective-permute-start(f32[10,1,1024]{2,1,0:T(1,128)S(1)} %get-tuple-element.36), channel_id=1, source_target_pairs={{0,4},{4,8},{8,12},{12,16},{16,20},{20,24},{24,28},{1,5},{5,9},{9,... | collective-permute-start | bytes 122888 | tf_op jit(solution)/shard_map/ppermute | solution.py:25
  267.0 2.0 convolution_bitcast_fusion
  270.3 6.3 %all-to-all-start.1 = ((f32[8,8,1024]{2,1,0:T(8,128)}), f32[8,8,1024]{2,1,0:T(8,128)}, u32[]{:S(2)}, u32[]{:S(2)}) async-start(f32[8,8,1024]{2,1,0:T(8,128)} %convolution_bitcast_fusion), calls=%async_computation.1 | async-start | bytes 524288 | tf_op jit(solution)/shard_map/all_to_all | solution.py:147
  276.6 0.7 fusion.85
  277.4 1.9 collective-permute-start.22
  279.3 1.3 collective-permute-start.23
  281.1 1.9 reduce.3
  283.0 1.3 eq.49
  284.7 2.1 concatenate.147
  286.8 3.4 fusion.70
  290.2 43.7 %all-reduce.6 = (f32[]{:T(128)}, f32[]{:T(128)}) all-reduce(f32[]{:T(128)} %get-tuple-element.16, f32[]{:T(128)} %fusion.70), channel_id=1, replica_groups=mesh['tiles'=8,'lev'=4] {'tiles','lev'}, use_global_device_ids=true, to_apply=%region_16.17 | all-reduce | flops 2 | bytes 16 | tf_op jit(solution)/shard_map/psum | solution.py:76
  337.4 1.2 convolution_bitcast_fusion.1
  339.3 0.9 multiply_add_fusion
  340.2 31.1 %all-reduce.12.cloned.1.call-done = f32[8,4096]{1,0:T(8,128)} async-done(((f32[8,4096]{1,0:T(8,128)}), f32[8,4096]{1,0:T(8,128)}) %all-reduce.12.cloned.1.call-update) | async-done | bytes 131088 | tf_op jit(solution)/shard_map/psum | solution.py:159
  371.3 1.6 copy.29
  (80 shorter events, 9.2 us)
Async XLA Ops:
  8.3 6.8 %collective-permute-start = (f32[10,1,1024]{2,1,0:T(1,128)S(1)}, f32[10,1,1024]{2,1,0:T(1,128)S(1)}, u32[]{:S(2)}, u32[]{:S(2)}) collective-permute-start(f32[10,1,1024]{2,1,0:T(1,128)S(1)} %get-tuple-element.47), channel_id=1, source_target_pairs={{4,0},{8,4},{12,8},{16,12},{20,16},{24,20},{28,24},{5,1},{9,5},{13... | collective-permute-start | bytes 122888 | tf_op jit(solution)/shard_map/ppermute | solution.py:27
  9.6 7.2 %collective-permute-start.1 = (f32[10,1,1024]{2,1,0:T(1,128)S(1)}, f32[10,1,1024]{2,1,0:T(1,128)S(1)}, u32[]{:S(2)}, u32[]{:S(2)}) collective-permute-start(f32[10,1,1024]{2,1,0:T(1,128)S(1)} %get-tuple-element.46), channel_id=1, source_target_pairs={{0,4},{4,8},{8,12},{12,16},{16,20},{20,24},{24,28},{1,5},{5,9},{9,... | collective-permute-start | bytes 122888 | tf_op jit(solution)/shard_map/ppermute | solution.py:25
  15.1 19.6 %copy-start.9 = (f32[10,1,1024]{2,1,0:T(1,128)}, f32[10,1,1024]{2,1,0:T(1,128)S(1)}, u32[]{:S(2)}) copy-start(f32[10,1,1024]{2,1,0:T(1,128)S(1)} %collective-permute-done) | copy-start | bytes 122884
  16.8 18.0 %copy-start.10 = (f32[10,1,1024]{2,1,0:T(1,128)}, f32[10,1,1024]{2,1,0:T(1,128)S(1)}, u32[]{:S(2)}) copy-start(f32[10,1,1024]{2,1,0:T(1,128)S(1)} %collective-permute-done.1) | copy-start | bytes 122884
  18.0 6.5 %collective-permute-start.2 = (f32[10,10,1]{2,1,0:T(8,128)S(1)}, f32[10,10,1]{2,1,0:T(8,128)S(1)}, u32[]{:S(2)}, u32[]{:S(2)}) collective-permute-start(f32[10,10,1]{2,1,0:T(8,128)S(1)} %get-tuple-element.34), channel_id=1, source_target_pairs={{1,0},{2,1},{3,2},{5,4},{6,5},{7,6},{9,8},{10,9},{11,10},{13,12},{... | collective-permute-start | bytes 1208 | tf_op jit(solution)/shard_map/ppermute | solution.py:27
  19.3 5.2 %collective-permute-start.3 = (f32[10,10,1]{2,1,0:T(8,128)S(1)}, f32[10,10,1]{2,1,0:T(8,128)S(1)}, u32[]{:S(2)}, u32[]{:S(2)}) collective-permute-start(f32[10,10,1]{2,1,0:T(8,128)S(1)} %get-tuple-element.35), channel_id=1, source_target_pairs={{0,1},{1,2},{2,3},{4,5},{5,6},{6,7},{8,9},{9,10},{10,11},{12,13},{... | collective-permute-start | bytes 1208 | tf_op jit(solution)/shard_map/ppermute | solution.py:25
  24.5 17.3 %copy-start.7 = (f32[10,10,1]{2,1,0:T(8,128)}, f32[10,10,1]{2,1,0:T(8,128)S(1)}, u32[]{:S(2)}) copy-start(f32[10,10,1]{2,1,0:T(8,128)S(1)} %collective-permute-done.2) | copy-start | bytes 1204
  24.5 17.3 %copy-start.8 = (f32[10,10,1]{2,1,0:T(8,128)}, f32[10,10,1]{2,1,0:T(8,128)S(1)}, u32[]{:S(2)}) copy-start(f32[10,10,1]{2,1,0:T(8,128)S(1)} %collective-permute-done.3) | copy-start | bytes 1204
  26.8 7.9 %collective-permute-start.4 = (f32[10,1,1024]{2,1,0:T(1,128)S(1)}, f32[10,1,1024]{2,1,0:T(1,128)S(1)}, u32[]{:S(2)}, u32[]{:S(2)}) collective-permute-start(f32[10,1,1024]{2,1,0:T(1,128)S(1)} %get-tuple-element.45), channel_id=1, source_target_pairs={{4,0},{8,4},{12,8},{16,12},{20,16},{24,20},{28,24},{5,1},{9,5},{13... | collective-permute-start | bytes 122888 | tf_op jit(solution)/shard_map/ppermute | solution.py:27
  28.1 7.6 %collective-permute-start.5 = (f32[10,1,1024]{2,1,0:T(1,128)S(1)}, f32[10,1,1024]{2,1,0:T(1,128)S(1)}, u32[]{:S(2)}, u32[]{:S(2)}) collective-permute-start(f32[10,1,1024]{2,1,0:T(1,128)S(1)} %get-tuple-element.44), channel_id=1, source_target_pairs={{0,4},{4,8},{8,12},{12,16},{16,20},{20,24},{24,28},{1,5},{5,9},{9,... | collective-permute-start | bytes 122888 | tf_op jit(solution)/shard_map/ppermute | solution.py:25
  34.7 6.6 %copy-start.14 = (s32[32]{0:T(128)}, s32[32]{0:T(128)S(1)}, u32[]{:S(2)}) copy-start(s32[32]{0:T(128)S(1)} %get-tuple-element.51) | copy-start | bytes 388
  34.7 5.5 %copy-start.3 = (f32[10,1,1024]{2,1,0:T(1,128)}, f32[10,1,1024]{2,1,0:T(1,128)S(1)}, u32[]{:S(2)}) copy-start(f32[10,1,1024]{2,1,0:T(1,128)S(1)} %collective-permute-done.4) | copy-start | bytes 122884
  35.6 4.6 %copy-start.5 = (f32[10,1,1024]{2,1,0:T(1,128)}, f32[10,1,1024]{2,1,0:T(1,128)S(1)}, u32[]{:S(2)}) copy-start(f32[10,1,1024]{2,1,0:T(1,128)S(1)} %collective-permute-done.5) | copy-start | bytes 122884
  35.9 5.5 %collective-permute-start.6 = (f32[10,10,1]{2,1,0:T(8,128)S(1)}, f32[10,10,1]{2,1,0:T(8,128)S(1)}, u32[]{:S(2)}, u32[]{:S(2)}) collective-permute-start(f32[10,10,1]{2,1,0:T(8,128)S(1)} %get-tuple-element.33), channel_id=1, source_target_pairs={{1,0},{2,1},{3,2},{5,4},{6,5},{7,6},{9,8},{10,9},{11,10},{13,12},{... | collective-permute-start | bytes 1208 | tf_op jit(solution)/shard_map/ppermute | solution.py:27
  37.2 4.2 %collective-permute-start.7 = (f32[10,10,1]{2,1,0:T(8,128)S(1)}, f32[10,10,1]{2,1,0:T(8,128)S(1)}, u32[]{:S(2)}, u32[]{:S(2)}) collective-permute-start(f32[10,10,1]{2,1,0:T(8,128)S(1)} %get-tuple-element.32), channel_id=1, source_target_pairs={{0,1},{1,2},{2,3},{4,5},{5,6},{6,7},{8,9},{9,10},{10,11},{12,13},{... | collective-permute-start | bytes 1208 | tf_op jit(solution)/shard_map/ppermute | solution.py:25
  41.4 0.6 copy-start.1
  45.4 90.2 %copy-start.2 = (f32[10,10,1]{2,1,0:T(8,128)S(1)}, f32[10,10,1]{2,1,0:T(8,128)}, u32[]{:S(2)}) copy-start(f32[10,10,1]{2,1,0:T(8,128)} %copy-done.1) | copy-start | bytes 1204
  45.4 90.2 %copy-start.4 = (f32[10,1,1024]{2,1,0:T(1,128)S(1)}, f32[10,1,1024]{2,1,0:T(1,128)}, u32[]{:S(2)}) copy-start(f32[10,1,1024]{2,1,0:T(1,128)} %copy-done.3) | copy-start | bytes 122884
  45.4 90.2 %copy-start.6 = (f32[10,1,1024]{2,1,0:T(1,128)S(1)}, f32[10,1,1024]{2,1,0:T(1,128)}, u32[]{:S(2)}) copy-start(f32[10,1,1024]{2,1,0:T(1,128)} %copy-done.5) | copy-start | bytes 122884
  45.5 7.4 %collective-permute-start.8 = (f32[10,1,1024]{2,1,0:T(1,128)S(1)}, f32[10,1,1024]{2,1,0:T(1,128)S(1)}, u32[]{:S(2)}, u32[]{:S(2)}) collective-permute-start(f32[10,1,1024]{2,1,0:T(1,128)S(1)} %get-tuple-element.43), channel_id=1, source_target_pairs={{4,0},{8,4},{12,8},{16,12},{20,16},{24,20},{28,24},{5,1},{9,5},{13... | collective-permute-start | bytes 122888 | tf_op jit(solution)/shard_map/ppermute | solution.py:27
  46.8 7.1 %collective-permute-start.9 = (f32[10,1,1024]{2,1,0:T(1,128)S(1)}, f32[10,1,1024]{2,1,0:T(1,128)S(1)}, u32[]{:S(2)}, u32[]{:S(2)}) collective-permute-start(f32[10,1,1024]{2,1,0:T(1,128)S(1)} %get-tuple-element.42), channel_id=1, source_target_pairs={{0,4},{4,8},{8,12},{12,16},{16,20},{20,24},{24,28},{1,5},{5,9},{9,... | collective-permute-start | bytes 122888 | tf_op jit(solution)/shard_map/ppermute | solution.py:25
  52.9 74.5 %copy-start.13 = (s32[32]{0:T(128)}, s32[32]{0:T(128)S(1)}, u32[]{:S(2)}) copy-start(s32[32]{0:T(128)S(1)} %multiply_add_fusion.2) | copy-start | bytes 388
  54.1 5.5 %collective-permute-start.10 = (f32[10,10,1]{2,1,0:T(8,128)S(1)}, f32[10,10,1]{2,1,0:T(8,128)S(1)}, u32[]{:S(2)}, u32[]{:S(2)}) collective-permute-start(f32[10,10,1]{2,1,0:T(8,128)S(1)} %get-tuple-element.31), channel_id=1, source_target_pairs={{0,1},{1,2},{2,3},{4,5},{5,6},{6,7},{8,9},{9,10},{10,11},{12,13},{... | collective-permute-start | bytes 1208 | tf_op jit(solution)/shard_map/ppermute | solution.py:25
  57.6 5.9 %collective-permute-start.11 = (f32[10,10,1]{2,1,0:T(8,128)S(1)}, f32[10,10,1]{2,1,0:T(8,128)S(1)}, u32[]{:S(2)}, u32[]{:S(2)}) collective-permute-start(f32[10,10,1]{2,1,0:T(8,128)S(1)} %get-tuple-element.30), channel_id=1, source_target_pairs={{1,0},{2,1},{3,2},{5,4},{6,5},{7,6},{9,8},{10,9},{11,10},{13,12},{... | collective-permute-start | bytes 1208 | tf_op jit(solution)/shard_map/ppermute | solution.py:27
  114.6 12.7 %collective-permute-start.12 = (f32[10,1,1024]{2,1,0:T(1,128)S(1)}, f32[10,1,1024]{2,1,0:T(1,128)S(1)}, u32[]{:S(2)}, u32[]{:S(2)}) collective-permute-start(f32[10,1,1024]{2,1,0:T(1,128)S(1)} %get-tuple-element.41), channel_id=1, source_target_pairs={{4,0},{8,4},{12,8},{16,12},{20,16},{24,20},{28,24},{5,1},{9,5},{13... | collective-permute-start | bytes 122888 | tf_op jit(solution)/shard_map/ppermute | solution.py:27
  115.9 11.4 %collective-permute-start.13 = (f32[10,1,1024]{2,1,0:T(1,128)S(1)}, f32[10,1,1024]{2,1,0:T(1,128)S(1)}, u32[]{:S(2)}, u32[]{:S(2)}) collective-permute-start(f32[10,1,1024]{2,1,0:T(1,128)S(1)} %get-tuple-element.40), channel_id=1, source_target_pairs={{0,4},{4,8},{8,12},{12,16},{16,20},{20,24},{24,28},{1,5},{5,9},{9,... | collective-permute-start | bytes 122888 | tf_op jit(solution)/shard_map/ppermute | solution.py:25
  121.4 148.9 %all-to-all-start = ((s32[8,1,8]{2,1,0:T(1,128)}), s32[8,1,8]{2,1,0:T(1,128)}, u32[]{:S(2)}, u32[]{:S(2)}) async-start(s32[8,1,8]{2,1,0:T(1,128)} %bitcast), calls=%async_computation | async-start | bytes 8192 | tf_op jit(solution)/shard_map/all_to_all | solution.py:148
  127.6 3.8 collective-permute-start.14
  128.9 5.5 %collective-permute-start.15 = (f32[10,10,1]{2,1,0:T(8,128)S(1)}, f32[10,10,1]{2,1,0:T(8,128)S(1)}, u32[]{:S(2)}, u32[]{:S(2)}) collective-permute-start(f32[10,10,1]{2,1,0:T(8,128)S(1)} %get-tuple-element.28), channel_id=1, source_target_pairs={{1,0},{2,1},{3,2},{5,4},{6,5},{7,6},{9,8},{10,9},{11,10},{13,12},{... | collective-permute-start | bytes 1208 | tf_op jit(solution)/shard_map/ppermute | solution.py:27
  186.2 8.2 %collective-permute-start.16 = (f32[10,1,1024]{2,1,0:T(1,128)S(1)}, f32[10,1,1024]{2,1,0:T(1,128)S(1)}, u32[]{:S(2)}, u32[]{:S(2)}) collective-permute-start(f32[10,1,1024]{2,1,0:T(1,128)S(1)} %get-tuple-element.39), channel_id=1, source_target_pairs={{4,0},{8,4},{12,8},{16,12},{20,16},{24,20},{28,24},{5,1},{9,5},{13... | collective-permute-start | bytes 122888 | tf_op jit(solution)/shard_map/ppermute | solution.py:27
  187.5 6.9 %collective-permute-start.17 = (f32[10,1,1024]{2,1,0:T(1,128)S(1)}, f32[10,1,1024]{2,1,0:T(1,128)S(1)}, u32[]{:S(2)}, u32[]{:S(2)}) collective-permute-start(f32[10,1,1024]{2,1,0:T(1,128)S(1)} %get-tuple-element.38), channel_id=1, source_target_pairs={{0,4},{4,8},{8,12},{12,16},{16,20},{20,24},{24,28},{1,5},{5,9},{9,... | collective-permute-start | bytes 122888 | tf_op jit(solution)/shard_map/ppermute | solution.py:25
  196.5 8.0 %collective-permute-start.18 = (f32[10,10,1]{2,1,0:T(8,128)S(1)}, f32[10,10,1]{2,1,0:T(8,128)S(1)}, u32[]{:S(2)}, u32[]{:S(2)}) collective-permute-start(f32[10,10,1]{2,1,0:T(8,128)S(1)} %get-tuple-element.27), channel_id=1, source_target_pairs={{0,1},{1,2},{2,3},{4,5},{5,6},{6,7},{8,9},{9,10},{10,11},{12,13},{... | collective-permute-start | bytes 1208 | tf_op jit(solution)/shard_map/ppermute | solution.py:25
  197.8 6.7 %collective-permute-start.19 = (f32[10,10,1]{2,1,0:T(8,128)S(1)}, f32[10,10,1]{2,1,0:T(8,128)S(1)}, u32[]{:S(2)}, u32[]{:S(2)}) collective-permute-start(f32[10,10,1]{2,1,0:T(8,128)S(1)} %get-tuple-element.26), channel_id=1, source_target_pairs={{1,0},{2,1},{3,2},{5,4},{6,5},{7,6},{9,8},{10,9},{11,10},{13,12},{... | collective-permute-start | bytes 1208 | tf_op jit(solution)/shard_map/ppermute | solution.py:27
  204.5 134.8 %copy-start = (f32[10,8,1024]{2,1,0:T(8,128)S(1)}, f32[10,8,1024]{2,1,0:T(8,128)}, u32[]{:S(2)}) copy-start(f32[10,8,1024]{2,1,0:T(8,128)} %param.21) | copy-start | bytes 983044
  260.9 8.1 %collective-permute-start.20 = (f32[10,1,1024]{2,1,0:T(1,128)S(1)}, f32[10,1,1024]{2,1,0:T(1,128)S(1)}, u32[]{:S(2)}, u32[]{:S(2)}) collective-permute-start(f32[10,1,1024]{2,1,0:T(1,128)S(1)} %get-tuple-element.37), channel_id=1, source_target_pairs={{4,0},{8,4},{12,8},{16,12},{20,16},{24,20},{28,24},{5,1},{9,5},{13... | collective-permute-start | bytes 122888 | tf_op jit(solution)/shard_map/ppermute | solution.py:27
  262.2 6.8 %collective-permute-start.21 = (f32[10,1,1024]{2,1,0:T(1,128)S(1)}, f32[10,1,1024]{2,1,0:T(1,128)S(1)}, u32[]{:S(2)}, u32[]{:S(2)}) collective-permute-start(f32[10,1,1024]{2,1,0:T(1,128)S(1)} %get-tuple-element.36), channel_id=1, source_target_pairs={{0,4},{4,8},{8,12},{12,16},{16,20},{20,24},{24,28},{1,5},{5,9},{9,... | collective-permute-start | bytes 122888 | tf_op jit(solution)/shard_map/ppermute | solution.py:25
  269.0 0.6 copy-start.11
  269.6 0.6 copy-start.12
  270.3 67.1 %all-to-all-start.1 = ((f32[8,8,1024]{2,1,0:T(8,128)}), f32[8,8,1024]{2,1,0:T(8,128)}, u32[]{:S(2)}, u32[]{:S(2)}) async-start(f32[8,8,1024]{2,1,0:T(8,128)} %convolution_bitcast_fusion), calls=%async_computation.1 | async-start | bytes 524288 | tf_op jit(solution)/shard_map/all_to_all | solution.py:147
  276.6 94.7 %all-reduce.12.cloned.1.call-start = ((), (), s32[]{:S(2)}) async-start(), calls=%async_computation.2 | async-start | bytes 262144 | tf_op jit(solution)/shard_map/psum | solution.py:159
  277.4 6.9 %collective-permute-start.22 = (f32[10,10,1]{2,1,0:T(8,128)}, f32[10,10,1]{2,1,0:T(8,128)}, u32[]{:S(2)}, u32[]{:S(2)}) collective-permute-start(f32[10,10,1]{2,1,0:T(8,128)} %get-tuple-element.25), channel_id=1, source_target_pairs={{0,1},{1,2},{2,3},{4,5},{5,6},{6,7},{8,9},{9,10},{10,11},{12,13},{... | collective-permute-start | bytes 1208 | tf_op jit(solution)/shard_map/ppermute | solution.py:25
  279.3 5.4 %collective-permute-start.23 = (f32[10,10,1]{2,1,0:T(8,128)}, f32[10,10,1]{2,1,0:T(8,128)}, u32[]{:S(2)}, u32[]{:S(2)}) collective-permute-start(f32[10,10,1]{2,1,0:T(8,128)} %get-tuple-element.24), channel_id=1, source_target_pairs={{1,0},{2,1},{3,2},{5,4},{6,5},{7,6},{9,8},{10,9},{11,10},{13,12},{... | collective-permute-start | bytes 1208 | tf_op jit(solution)/shard_map/ppermute | solution.py:27
Sparse Core Ops, SparseCore 0:
  339.4 31.8 all-reduce.11
where the time goes:
time: 382 us; the launch traced here: 380 us
  blocking collectives  176 us (46%)
  starting transfers between devices  72.7 us (19%)
  waiting for transfers between devices  42 us (11%)
  other arithmetic  34 us (9%)
  between operations  27.8 us (7%)
  local copies, waits for them, and re-layouts  18.5 us (5%)
  matrix products  8.41 us (2%)
    psum x4, blocking collectives, paired_totals(): lax.psum((jnp.sum(residual * residual), jnp.sum(residual * image)), ('til...  176 us
    ppermute x12, starting transfers between devices, extended(): lax.ppermute(tail, axis, [(i, (i + 1) % count) for i in range(ends)])  44.9 us
    psum x1, waiting for transfers between devices, body(): totals = lax.psum(partial_sums, 'lev')  31.1 us
    ppermute x12, starting transfers between devices, extended(): lax.ppermute(head, axis, [((i + 1) % count, i) for i in range(ends)])  15.7 us
    reduce_sum x4, other arithmetic, paired_totals(): jnp.sum(residual * image)  14 us
  transfers between devices with their start and end apart: 27, of which 7 were waited for; matrix products, arithmetic and copies ran while one was open for 11% of the time, Pallas kernels for 0%

commit v1 on v0

v1 whole, which is shorter than its diff:
```python
import functools

import jax
import jax.numpy as jnp
from jax import lax
from jax.experimental import pallas as pl
from jax.experimental.pallas import tpu as pltpu
from jax.sharding import PartitionSpec as P

ITERS = 4
VISC_FLOOR = 0.25
VERTICAL = 4.0
SMB_WEIGHT = 0.5
SIGMA = 10.0
LANES = 128
MESH = pl.DeviceIdType.MESH
F32 = jnp.float32


def kernel(
    T, Q, cap, tpd,
    land, wts, btile, bland, bclass, mask, thk, prev, fric, drv, vel,
    tot_out, vel_out,
    v_e, drv_e, thk_e, prev_e, fric_e, mask_e,
    s_f, d_f, w_f, k_f,
    vsu, vsd, vrt, vrb, su, sd, rt, rb, sht, shb,
    dots, g_send, g_lev, g_mid, g_til,
    wbuf, lbuf, idx_m, tile_m, payload, rec, part, rs_rec, tot_s,
    loc_sem, w_sem, col_ss, col_rs, row_ss, row_rs, v_ss, v_rs,
    gl_ss, gl_rs, gt_ss, gt_rs, a_ss, a_rs, r_ss, r_rs, t_ss, t_rs,
):
    mt = lax.axis_index("tiles")
    ml = lax.axis_index("lev")
    levels, rows, cols = vel.shape
    wide = cols + 2 * LANES
    nblk = wts.shape[0]
    cells = wts.shape[2]
    inv_sigma = 1.0 / SIGMA

    def remote(src, dst, ss, rs, **where):
        return pltpu.make_async_remote_copy(
            src_ref=src, dst_ref=dst, send_sem=ss, recv_sem=rs,
            device_id=where, device_id_type=MESH)

    raw = (vel, drv, thk, prev, fric, mask)
    ext = (v_e, drv_e, thk_e, prev_e, fric_e, mask_e)

    def mid(ref):
        return ref.at[..., pl.ds(LANES, cols)]

    for k in range(6):
        pltpu.make_async_copy(raw[k], mid(ext[k]), loc_sem.at[k]).start()
    nchunk = w_sem.shape[0]
    per = nblk // nchunk
    for c in range(nchunk):
        pltpu.make_async_copy(wts.at[pl.ds(c * per, per)], wbuf.at[pl.ds(c * per, per)], w_sem.at[c]).start()

    bar = pltpu.get_barrier_semaphore()
    for d in range(1, Q):
        pl.semaphore_signal(bar, inc=1, device_id={"lev": lax.rem(ml + d, Q)}, device_id_type=MESH)
    for d in range(1, T):
        pl.semaphore_signal(bar, inc=1, device_id={"tiles": lax.rem(mt + d, T)}, device_id_type=MESH)

    s_f[0] = jnp.zeros((rows, wide), F32)
    s_f[levels + 1] = jnp.zeros((rows, wide), F32)
    w_f[0] = jnp.zeros((rows, wide), F32)
    w_f[levels + 1] = jnp.zeros((rows, wide), F32)

    @pl.when(mt == 0)
    def _():
        vrt[...] = jnp.zeros(vrt.shape, F32)
        rt[...] = jnp.zeros(rt.shape, F32)

    @pl.when(mt == T - 1)
    def _():
        vrb[...] = jnp.zeros(vrb.shape, F32)
        rb[...] = jnp.zeros(rb.shape, F32)

    for ref in ext:
        @pl.when(ml == 0)
        def _():
            ref[..., 0:LANES] = jnp.zeros(ref.shape[:-1] + (LANES,), ref.dtype)

        @pl.when(ml == Q - 1)
        def _():
            ref[..., LANES + cols:] = jnp.zeros(ref.shape[:-1] + (LANES,), ref.dtype)

    pl.semaphore_wait(bar, Q - 1 + T - 1)

    def col_right(k):
        return remote(raw[k].at[..., pl.ds(cols - LANES, LANES)], ext[k].at[..., pl.ds(0, LANES)],
                      col_ss.at[k, 0], col_rs.at[k, 0], lev=ml + 1)

    def col_left(k):
        return remote(raw[k].at[..., pl.ds(0, LANES)], ext[k].at[..., pl.ds(LANES + cols, LANES)],
                      col_ss.at[k, 1], col_rs.at[k, 1], lev=ml - 1)

    @pl.when(ml < Q - 1)
    def _():
        for k in (0, 5, 1, 2, 3, 4):
            col_right(k).start()

    @pl.when(ml > 0)
    def _():
        for k in (0, 5, 1, 2, 3, 4):
            col_left(k).start()

    def col_wait(ks):
        for k in ks:
            pltpu.make_async_copy(raw[k], mid(ext[k]), loc_sem.at[k]).wait()

        @pl.when(ml > 0)
        def _():
            for k in ks:
                col_right(k).wait_recv()

        @pl.when(ml < Q - 1)
        def _():
            for k in ks:
                col_left(k).wait_recv()

    classes = land.shape[1]
    stride = lbuf.shape[0] // land.shape[0]
    lbuf[...] = jnp.zeros(lbuf.shape, lbuf.dtype)
    for i in range(land.shape[0]):
        lbuf[stride * i:stride * i + classes, :] = land[i].astype(F32)
    for b in range(nblk):
        idx_m[b:b + 1, :] = jnp.full((1, idx_m.shape[1]), bland[b] * stride + bclass[b], jnp.int32)
        tile_m[b:b + 1, :] = jnp.full((1, LANES), btile[b], jnp.int32)
    pick_hot = (idx_m[...] == lax.broadcasted_iota(jnp.int32, idx_m.shape, 1)).astype(jnp.bfloat16)
    picked = jnp.dot(pick_hot, lbuf[...].astype(jnp.bfloat16), preferred_element_type=F32)
    tiles_b = tile_m[...]
    dest = tiles_b // tpd
    sub = lax.broadcasted_iota(jnp.int32, (nblk, LANES), 0)
    lane = lax.broadcasted_iota(jnp.int32, (nblk, LANES), 1)
    dest_row = jnp.sum(jnp.where(sub == lane, dest, 0), axis=0, keepdims=True)
    rank = jnp.sum(jnp.where(jnp.logical_and(dest == dest_row, lane < sub), 1.0, 0.0), axis=1, keepdims=True)
    slot = dest * cap + rank.astype(jnp.int32)
    local_id = (tiles_b % tpd + 1).astype(F32)
    nslot = T * cap
    slot_iota = lax.broadcasted_iota(jnp.int32, (nslot, LANES), 0)
    ids = jnp.zeros((nslot, LANES), F32)
    lhs = []
    for b in range(nblk):
        hit = slot_iota == slot[b:b + 1, :]
        ids = ids + jnp.where(hit, local_id[b:b + 1, :], 0.0)
        lhs.append(jnp.where(hit, picked[b:b + 1, :], 0.0).astype(jnp.bfloat16))

    col_wait((0, 5))
    for l in range(levels):
        x = v_e[l]
        vsu[l:l + 1, :] = x[0:1, :]
        vsu[levels + l:levels + l + 1, :] = x[1:2, :]
        vsd[l:l + 1, :] = x[rows - 1:rows, :]
        vsd[levels + l:levels + l + 1, :] = x[rows - 2:rows - 1, :]
    frac = mask_e[...].astype(F32)
    vsu[2 * levels:2 * levels + 1, :] = frac[0:1, :]
    vsd[2 * levels:2 * levels + 1, :] = frac[rows - 1:rows, :]

    def v_up():
        return remote(vsu, vrb, v_ss.at[0], v_rs.at[0], tiles=mt - 1)

    def v_down():
        return remote(vsd, vrt, v_ss.at[1], v_rs.at[1], tiles=mt + 1)

    @pl.when(mt > 0)
    def _():
        v_up().start()

    @pl.when(mt < T - 1)
    def _():
        v_down().start()

    acc = jnp.zeros((nslot, cells), F32)
    for c in range(nchunk):
        pltpu.make_async_copy(wts.at[pl.ds(c * per, per)], wbuf.at[pl.ds(c * per, per)], w_sem.at[c]).wait()
        left = jnp.concatenate(lhs[c * per:(c + 1) * per], axis=1)
        right = wbuf[c * per:(c + 1) * per].reshape(per * LANES, cells)
        acc = acc + jnp.dot(left, right, preferred_element_type=F32)
    for t in range(T):
        payload[t, :, 0:cells] = acc[t * cap:(t + 1) * cap, :]
        payload[t, :, cells:] = ids[t * cap:(t + 1) * cap, :]

    col_wait((1, 2, 3, 4))

    @pl.when(mt < T - 1)
    def _():
        v_up().wait_recv()

    @pl.when(mt > 0)
    def _():
        v_down().wait_recv()

    def a2a(d):
        to = lax.rem(mt + d, T)
        return remote(payload.at[to], rec.at[d - 1], a_ss.at[d - 1], a_rs.at[d - 1], tiles=to)

    for d in range(1, T):
        a2a(d).start()

    row_id = lax.broadcasted_iota(jnp.int32, (rows, wide), 0)

    def around(x, top, bot):
        after = jnp.where(row_id == rows - 1, bot, pltpu.roll(x, rows - 1, 0))
        before = jnp.where(row_id == 0, top, pltpu.roll(x, 1, 0))
        return before, after, pltpu.roll(x, 1, 1), pltpu.roll(x, wide - 1, 1)

    root = SIGMA ** -0.5

    def s_from(dx, dy, fr):
        q = VISC_FLOOR + 0.25 * (dx * dx) + 0.25 * (dy * dy)
        return fr * (root * jnp.exp(jnp.log(q) * (-1.0 / 6.0)))

    near_t, far_t = vrt[0:levels, :], vrt[levels:2 * levels, :]
    near_b, far_b = vrb[0:levels, :], vrb[levels:2 * levels, :]
    own_t, own_b = vsu[0:levels, :], vsd[0:levels, :]
    sht[...] = s_from(own_t - far_t, pltpu.roll(near_t, wide - 1, 1) - pltpu.roll(near_t, 1, 1),
                      vrt[2 * levels:2 * levels + 1, :])
    shb[...] = s_from(far_b - own_b, pltpu.roll(near_b, wide - 1, 1) - pltpu.roll(near_b, 1, 1),
                      vrb[2 * levels:2 * levels + 1, :])

    def s_level(l, carry):
        x = v_e[l]
        before, after, low, high = around(x, vrt[pl.ds(l, 1), :], vrb[pl.ds(l, 1), :])
        s = s_from(after - before, high - low, frac)
        s_f[l + 1] = s
        w_f[l + 1] = s * x
        return carry

    lax.fori_loop(0, levels, s_level, 0)

    def total(ref, l, top, bot):
        before, after, low, high = around(ref[l + 1], top, bot)
        return ((before + after) + (low + high)) + VERTICAL * (ref[l] + ref[l + 2])

    drag = frac * fric_e[...] + (1.0 - frac)
    drag_s = drag * inv_sigma - 1.0
    coef = frac * (thk_e[...] + SMB_WEIGHT * prev_e[...])

    def start_level(l, carry):
        st, sb = sht[pl.ds(l, 1), :], shb[pl.ds(l, 1), :]
        s = s_f[l + 1]
        diag = drag_s + s * total(s_f, l, st, sb)
        d_f[l] = diag
        x = v_e[l]
        image = (diag + 1.0) * x - s * total(w_f, l, st * vrt[pl.ds(l, 1), :], sb * vrb[pl.ds(l, 1), :])
        r = coef * drv_e[l] - SIGMA * image
        k_f[0, l] = r
        w = s * r
        su[0, pl.ds(l, 1), :] = w[0:1, :]
        sd[0, pl.ds(l, 1), :] = w[rows - 1:rows, :]
        return carry

    lax.fori_loop(0, levels, start_level, 0)

    def row_up(k):
        return remote(su.at[k], rb.at[k], row_ss.at[k, 0], row_rs.at[k, 0], tiles=mt - 1)

    def row_down(k):
        return remote(sd.at[k], rt.at[k], row_ss.at[k, 1], row_rs.at[k, 1], tiles=mt + 1)

    def row_start(k):
        @pl.when(mt > 0)
        def _():
            row_up(k).start()

        @pl.when(mt < T - 1)
        def _():
            row_down(k).start()

    def row_wait(k):
        @pl.when(mt < T - 1)
        def _():
            row_up(k).wait_recv()

        @pl.when(mt > 0)
        def _():
            row_down(k).wait_recv()

    def tile_sums():
        for d in range(1, T):
            a2a(d).wait_recv()
        rec[T - 1] = payload[mt]
        every = rec[...].reshape(T * cap, cells + LANES)
        hot = (every[:, cells:] == (lax.broadcasted_iota(jnp.int32, (T * cap, LANES), 1) + 1).astype(F32)).astype(F32)
        sums = lax.dot_general(hot, every[:, 0:cells], (((0,), (0,)), ((), ())),
                               precision=lax.Precision.HIGHEST, preferred_element_type=F32)
        share = cells // Q
        for q in range(Q):
            part[q] = sums[0:tpd, q * share:(q + 1) * share]
        for d in range(1, Q):
            scatter(d).start()

    def scatter(d):
        to = lax.rem(ml + d, Q)
        return remote(part.at[to], rs_rec.at[d - 1], r_ss.at[d - 1], r_rs.at[d - 1], lev=to)

    def gather(d, slot_of):
        return remote(tot_s.at[slot_of], tot_s.at[slot_of], t_ss.at[d - 1], t_rs.at[d - 1], lev=lax.rem(ml + d, Q))

    def lev_sums():
        value = part[ml]
        for d in range(1, Q):
            scatter(d).wait_recv()
            value = value + rs_rec[d - 1]
        tot_s[ml] = value
        for d in range(1, Q):
            gather(d, ml).start()

    own = slice(LANES, LANES + cols)

    def fold(x):
        return jnp.sum(x[:, own], axis=0, keepdims=True)

    for k in range(ITERS):
        row_start(k)

        def w_level(l, carry):
            w_f[l + 1] = s_f[l + 1] * k_f[k, l]
            return carry

        lax.fori_loop(0, levels, w_level, 0)
        if k == 1:
            tile_sums()
        if k == 3:
            lev_sums()
        row_wait(k)

        def step_level(l, carry):
            now, cross = carry
            s = s_f[l + 1]
            v = k_f[k, l]
            nxt = d_f[l] * v - s * total(w_f, l, rt[k, pl.ds(l, 1), :], rb[k, pl.ds(l, 1), :])
            if k + 1 < ITERS:
                k_f[k + 1, l] = nxt
                w = s * nxt
                su[k + 1, pl.ds(l, 1), :] = w[0:1, :]
                sd[k + 1, pl.ds(l, 1), :] = w[rows - 1:rows, :]
            v, nxt = v[:, own], nxt[:, own]
            return now + v * v, cross + v * nxt

        zero = jnp.zeros((rows, cols), F32)
        now, cross = lax.fori_loop(0, levels, step_level, (zero, zero))
        for j, value in ((2 * k, now), (2 * k + 1, cross)):
            line = jnp.sum(value, axis=0, keepdims=True)
            piece = line[:, 0:LANES]
            for i in range(1, cols // LANES):
                piece = piece + line[:, i * LANES:(i + 1) * LANES]
            g_send[j:j + 1, :] = piece

    def g_lev_copy(d):
        return remote(g_send, g_lev.at[d - 1], gl_ss.at[d - 1], gl_rs.at[d - 1], lev=lax.rem(ml + d, Q))

    def g_til_copy(d):
        return remote(g_mid, g_til.at[d - 1], gt_ss.at[d - 1], gt_rs.at[d - 1], tiles=lax.rem(mt + d, T))

    for d in range(1, Q):
        g_lev_copy(d).start()
    value = g_send[...]
    for d in range(1, Q):
        g_lev_copy(d).wait_recv()
        value = value + g_lev[d - 1]
    g_mid[...] = value
    for d in range(1, T):
        g_til_copy(d).start()
    for d in range(1, Q):
        gather(d, lax.rem(ml - d + Q, Q)).wait_recv()
    tot_out[...] = tot_s[...]
    for d in range(1, T):
        g_til_copy(d).wait_recv()
        value = value + g_til[d - 1]
    summed = jnp.broadcast_to(jnp.sum(value, axis=1, keepdims=True), value.shape)
    mu = [summed[j:j + 1, :] for j in range(2 * ITERS)]

    def inner(a, b):
        out = None
        for i, ai in enumerate(a):
            for j, bj in enumerate(b):
                if ai is None or bj is None:
                    continue
                term = ai * bj * mu[i + j]
                out = term if out is None else out + term
        return out

    one = jnp.ones((1, LANES), F32)
    nil = jnp.zeros((1, LANES), F32)
    res = [one]
    direc = [one]
    sol = [nil] * ITERS
    rr = mu[0]
    for it in range(ITERS):
        img = [SIGMA * ((direc[i] if i < len(direc) else nil) + (direc[i - 1] if i > 0 else nil))
               for i in range(len(direc) + 1)]
        alpha = rr / inner(direc, img)
        for i in range(len(direc)):
            sol[i] = sol[i] + alpha * direc[i]
        if it + 1 == ITERS:
            break
        res = [(res[i] if i < len(res) else nil) - alpha * img[i] for i in range(len(img))]
        new = inner(res, res)
        beta = new / rr
        direc = [res[i] + beta * (direc[i] if i < len(direc) else nil) for i in range(len(res))]
        rr = new
    wide_sol = [jnp.concatenate([jnp.broadcast_to(c, (rows, LANES))] * (cols // LANES), axis=1) for c in sol]

    def end_level(l, carry):
        x = v_e[l][:, own]
        for k in range(ITERS):
            x = x + wide_sol[k] * k_f[k, l][:, own]
        vel_out[l] = x
        return carry

    lax.fori_loop(0, levels, end_level, 0)

    @pl.when(ml < Q - 1)
    def _():
        for k in range(6):
            col_right(k).wait_send()

    @pl.when(ml > 0)
    def _():
        for k in range(6):
            col_left(k).wait_send()

    @pl.when(mt > 0)
    def _():
        v_up().wait_send()
        for k in range(ITERS):
            row_up(k).wait_send()

    @pl.when(mt < T - 1)
    def _():
        v_down().wait_send()
        for k in range(ITERS):
            row_down(k).wait_send()

    for d in range(1, T):
        a2a(d).wait_send()
        g_til_copy(d).wait_send()
    for d in range(1, Q):
        scatter(d).wait_send()
        gather(d, ml).wait_send()
        g_lev_copy(d).wait_send()


def body(T, Q, land_smb, block_weights, block_tile, block_land, block_class, ice_mask,
         thickness, prev_smb, basal_friction, driving, velocity_start):
    levels, rows, cols = velocity_start.shape
    nblk, land_cols, cells = block_weights.shape
    wide = cols + 2 * LANES
    tpd = cols * Q // LANES
    cap = max(2, 2 * nblk // T)
    cap = -(-cap // 8) * 8
    stride = -(-land_smb.shape[1] // 16) * 16
    lrows = -(-land_smb.shape[0] * stride // LANES) * LANES
    share = cells // Q
    dma = pltpu.SemaphoreType.DMA
    vm = pl.BlockSpec(memory_space=pltpu.VMEM)
    sm = pl.BlockSpec(memory_space=pltpu.SMEM)
    anyw = pl.BlockSpec(memory_space=pl.ANY)

    def f(*shape):
        return pltpu.VMEM(shape, F32)

    totals, velocity = pl.pallas_call(
        functools.partial(kernel, T, Q, cap, tpd),
        out_shape=(jax.ShapeDtypeStruct((Q, tpd, share), F32),
                   jax.ShapeDtypeStruct(velocity_start.shape, F32)),
        in_specs=[vm, anyw, sm, sm, sm] + [anyw] * 6,
        out_specs=(vm, vm),
        scratch_shapes=[
            f(levels, rows, wide), f(levels, rows, wide), f(rows, wide), f(rows, wide), f(rows, wide),
            pltpu.VMEM((rows, wide), jnp.int32),
            f(levels + 2, rows, wide), f(levels, rows, wide), f(levels + 2, rows, wide),
            f(ITERS, levels, rows, wide),
            f(2 * levels + 1, wide), f(2 * levels + 1, wide), f(2 * levels + 1, wide), f(2 * levels + 1, wide),
            f(ITERS, levels, wide), f(ITERS, levels, wide), f(ITERS, levels, wide), f(ITERS, levels, wide),
            f(levels, wide), f(levels, wide),
            f(8, LANES), f(2 * ITERS, LANES), f(Q - 1, 2 * ITERS, LANES), f(2 * ITERS, LANES),
            f(T - 1, 2 * ITERS, LANES),
            pltpu.VMEM(block_weights.shape, block_weights.dtype),
            f(lrows, LANES), pltpu.VMEM((nblk, lrows), jnp.int32), pltpu.VMEM((nblk, LANES), jnp.int32),
            f(T, cap, cells + LANES), f(T, cap, cells + LANES),
            f(Q, tpd, share), f(Q - 1, tpd, share), f(Q, tpd, share),
            dma((6,)), dma((4,)), dma((6, 2)), dma((6, 2)), dma((ITERS, 2)), dma((ITERS, 2)), dma((2,)), dma((2,)),
            dma((Q - 1,)), dma((Q - 1,)), dma((T - 1,)), dma((T - 1,)), dma((T - 1,)), dma((T - 1,)),
            dma((Q - 1,)), dma((Q - 1,)), dma((Q - 1,)), dma((Q - 1,)),
        ],
        compiler_params=pltpu.CompilerParams(collective_id=0, has_side_effects=True,
                                             vmem_limit_bytes=60 * 1024 * 1024),
        name="remap_and_solve",
    )(land_smb, block_weights, block_tile, block_land, block_class, ice_mask, thickness, prev_smb,
      basal_friction, driving, velocity_start)
    per = share // LANES
    ice_smb = totals.reshape(Q, tpd, per, LANES).transpose(0, 2, 1, 3).reshape(rows, tpd * LANES)
    return ice_smb, velocity


def solution(mesh):
    T, Q = mesh.shape["tiles"], mesh.shape["lev"]
    both = P(("tiles", "lev"))
    in_specs = (both, both, both, both, both) + (P("tiles", "lev"),) * 4 + (P(None, "tiles", "lev"),) * 2
    out_specs = (P("tiles", None), P(None, "tiles", "lev"))
    return jax.shard_map(functools.partial(body, T, Q), mesh=mesh, in_specs=in_specs,
                         out_specs=out_specs, check_vma=False)
```

time: 382 us -> 57.3 us (0.15)
  blocking collectives: 176 us -> 0 us
  starting transfers between devices: 72.7 us -> 0 us
  Pallas kernels: 0 us -> 51.5 us
  waiting for transfers between devices: 42 us -> 0 us
  other arithmetic: 34 us -> 0 us
  between operations: 27.8 us -> 0.65 us
  local copies, waits for them, and re-layouts: 18.5 us -> 4.86 us
  matrix products: 8.41 us -> 0 us
    psum x4 -> x0, blocking collectives: 176 us -> none  [paired_totals(): lax.psum((jnp.sum(residual * residual), jnp.sum(residual * image)), ('til...]
    ppermute x24 -> x0, starting transfers between devices: 60.5 us -> none  [the longest x12 44.9 us: extended(): lax.ppermute(tail, axis, [(i, (i + 1) % count) for i in range(ends)])]
    pallas_call x0 -> x1, Pallas kernels: none -> 51.5 us  [body(): pl.pallas_call(functools.partial(kernel, T, Q, cap, tpd), out_shape=(jax....]
    psum x1 -> x0, waiting for transfers between devices: 31.1 us -> none  [body(): totals = lax.psum(partial_sums, 'lev')]
    reduce_sum x7 -> x0, other arithmetic: 17.2 us -> none  [the longest x4 14 us: paired_totals(): jnp.sum(residual * image)]
    all_to_all x2 -> x0, starting transfers between devices: 12.2 us -> none  [the longest x1 6.25 us: body(): lax.all_to_all(sending, 'tiles', split_axis=0, concat_axis=0, tiled=True)]
    ppermute x24 -> x0, waiting for transfers between devices: 10.9 us -> none  [the longest x12 7.37 us: extended(): lax.ppermute(head, axis, [((i + 1) % count, i) for i in range(ends)])]
    dot_general x3 -> x0, matrix products: 8.41 us -> none  [the longest x1 5.24 us: body(): jnp.einsum('bl,blt->bt', picked, block_weights, preferred_element_type=jn...]
  transfers between devices with their start and end apart: 27 -> 0, of which waited for: 7 -> 0; matrix products, arithmetic and copies ran while one was open for 11% -> 0% of each run, Pallas kernels for 0% -> 0%
where the time goes in v1:
time: 57.3 us; the launch traced here: 57.1 us
  Pallas kernels  51.5 us (90%)
  local copies, waits for them, and re-layouts  4.86 us (8%)
  between operations  0.65 us (1%)
    pallas_call x1, Pallas kernels, body(): pl.pallas_call(functools.partial(kernel, T, Q, cap, tpd), out_shape=(jax....  51.5 us
    unnamed x3, local copies, waits for them, and re-layouts  3.88 us

profile of v1, /device:TPU:0, one launch (start us, length us, event | category | flops | bytes accessed | tf_op | source)
XLA Modules:
  0.0 57.1 jit_solution(13467326857159873425)
XLA Ops:
  0.6 1.4 %copy.13.land = bf16[16,10,128]{2,1,0:T(8,128)(2,1)} copy(bf16[16,10,128]{2,0,1:T(8,128)(2,1)} %param.11) | data formatting | bytes 81920 | tf_op args[0]
  2.1 51.5 %remap_and_solve.1 = (f32[4,32,256]{2,1,0:T(8,128)}, f32[10,8,1024]{2,1,0:T(8,128)}) custom-call(bf16[16,10,128]{2,1,0:T(8,128)(2,1)} %copy.13.land, bf16[32,128,1024]{2,1,0:T(8,128)(2,1)} %wts.1, s32[32]{0:T(128)} %btile.1, s32[32]{0:T(128)} %bland.1, s32[32]{0:T(128)} %bclass.1, s32[8,1024]{1,0:T(8,128)} %mask.1, f32[8,1024]{1,0:T(8,128)} %thk.1, ...), custom_call_target="tpu_custom_call" | custom-call | tf_op jit(solution)/shard_map/remap_and_solve/pallas_call | solution.py:465
  53.6 1.0 %reshape.10 = f32[4,32,2,128]{3,2,1,0:T(2,128)S(1)} reshape(f32[4,32,256]{2,1,0:T(8,128)} %get-tuple-element.4) | data formatting | bytes 262144 | tf_op jit(solution)/shard_map/reshape | solution.py:495
  54.6 0.7 %copy.17 = f32[1,8,32,128]{3,1,2,0:T(8,128)} copy(f32[1,8,32,128]{3,2,1,0:T(8,128)S(1)} %bitcast.7) | data formatting | bytes 262144
  55.3 1.7 %copy.19 = f32[10,8,1024]{2,1,0:T(8,128)} copy(f32[10,8,1024]{2,1,0:T(8,128)} %get-tuple-element.9) | data formatting | bytes 655360
  (1 shorter events, 0.0 us)

commit v2 on v1

--- a/solution.py
+++ b/solution.py
@@ -24,7 +24,8 @@
     v_e, drv_e, thk_e, prev_e, fric_e, mask_e,
     s_f, d_f, w_f, k_f,
     vsu, vsd, vrt, vrb, su, sd, rt, rb, sht, shb,
-    dots, g_send, g_lev, g_mid, g_til,
+    o_t, i_t, i_b, o_b, se_t, se_b, pe_t, pe_b, ve_t, ve_b,
+    g_send, g_lev, g_mid, g_til,
     wbuf, lbuf, idx_m, tile_m, payload, rec, part, rs_rec, tot_s,
     loc_sem, w_sem, col_ss, col_rs, row_ss, row_rs, v_ss, v_rs,
     gl_ss, gl_rs, gt_ss, gt_rs, a_ss, a_rs, r_ss, r_rs, t_ss, t_rs,
@@ -61,6 +62,11 @@
     for d in range(1, T):
         pl.semaphore_signal(bar, inc=1, device_id={"tiles": lax.rem(mt + d, T)}, device_id_type=MESH)
 
+    for i in (1, T - 1):
+        for j in (1, Q - 1):
+            pl.semaphore_signal(bar, inc=1, device_id={"tiles": lax.rem(mt + i, T), "lev": lax.rem(ml + j, Q)},
+                                device_id_type=MESH)
+
     s_f[0] = jnp.zeros((rows, wide), F32)
     s_f[levels + 1] = jnp.zeros((rows, wide), F32)
     w_f[0] = jnp.zeros((rows, wide), F32)
@@ -85,47 +91,12 @@
         def _():
             ref[..., LANES + cols:] = jnp.zeros(ref.shape[:-1] + (LANES,), ref.dtype)
 
-    pl.semaphore_wait(bar, Q - 1 + T - 1)
-
-    def col_right(k):
-        return remote(raw[k].at[..., pl.ds(cols - LANES, LANES)], ext[k].at[..., pl.ds(0, LANES)],
-                      col_ss.at[k, 0], col_rs.at[k, 0], lev=ml + 1)
-
-    def col_left(k):
-        return remote(raw[k].at[..., pl.ds(0, LANES)], ext[k].at[..., pl.ds(LANES + cols, LANES)],
-                      col_ss.at[k, 1], col_rs.at[k, 1], lev=ml - 1)
-
-    @pl.when(ml < Q - 1)
-    def _():
-        for k in (0, 5, 1, 2, 3, 4):
-            col_right(k).start()
-
-    @pl.when(ml > 0)
-    def _():
-        for k in (0, 5, 1, 2, 3, 4):
-            col_left(k).start()
-
-    def col_wait(ks):
-        for k in ks:
-            pltpu.make_async_copy(raw[k], mid(ext[k]), loc_sem.at[k]).wait()
-
-        @pl.when(ml > 0)
-        def _():
-            for k in ks:
-                col_right(k).wait_recv()
-
-        @pl.when(ml < Q - 1)
-        def _():
-            for k in ks:
-                col_left(k).wait_recv()
-
-    classes = land.shape[1]
-    stride = lbuf.shape[0] // land.shape[0]
+    classes, lands = land.shape[0], land.shape[1]
     lbuf[...] = jnp.zeros(lbuf.shape, lbuf.dtype)
-    for i in range(land.shape[0]):
-        lbuf[stride * i:stride * i + classes, :] = land[i].astype(F32)
+    for i in range(classes):
+        lbuf[lands * i:lands * (i + 1), :] = land[i].astype(F32)
     for b in range(nblk):
-        idx_m[b:b + 1, :] = jnp.full((1, idx_m.shape[1]), bland[b] * stride + bclass[b], jnp.int32)
+        idx_m[b:b + 1, :] = jnp.full((1, idx_m.shape[1]), bclass[b] * lands + bland[b], jnp.int32)
         tile_m[b:b + 1, :] = jnp.full((1, LANES), btile[b], jnp.int32)
     pick_hot = (idx_m[...] == lax.broadcasted_iota(jnp.int32, idx_m.shape, 1)).astype(jnp.bfloat16)
     picked = jnp.dot(pick_hot, lbuf[...].astype(jnp.bfloat16), preferred_element_type=F32)
@@ -146,30 +117,84 @@
         ids = ids + jnp.where(hit, local_id[b:b + 1, :], 0.0)
         lhs.append(jnp.where(hit, picked[b:b + 1, :], 0.0).astype(jnp.bfloat16))
 
-    col_wait((0, 5))
+    def load_wait(ks):
+        for k in ks:
+            pltpu.make_async_copy(raw[k], mid(ext[k]), loc_sem.at[k]).wait()
+
+    own = slice(LANES, LANES + cols)
+    load_wait((0, 5))
     for l in range(levels):
-        x = v_e[l]
+        x = v_e[l, :, LANES:LANES + cols]
         vsu[l:l + 1, :] = x[0:1, :]
         vsu[levels + l:levels + l + 1, :] = x[1:2, :]
         vsd[l:l + 1, :] = x[rows - 1:rows, :]
         vsd[levels + l:levels + l + 1, :] = x[rows - 2:rows - 1, :]
-    frac = mask_e[...].astype(F32)
+    frac = mask_e[:, own].astype(F32)
     vsu[2 * levels:2 * levels + 1, :] = frac[0:1, :]
     vsd[2 * levels:2 * levels + 1, :] = frac[rows - 1:rows, :]
 
-    def v_up():
-        return remote(vsu, vrb, v_ss.at[0], v_rs.at[0], tiles=mt - 1)
-
-    def v_down():
-        return remote(vsd, vrt, v_ss.at[1], v_rs.at[1], tiles=mt + 1)
-
-    @pl.when(mt > 0)
-    def _():
-        v_up().start()
-
-    @pl.when(mt < T - 1)
-    def _():
-        v_down().start()
+    pl.semaphore_wait(bar, Q - 1 + T - 1 + 4)
+
+    def col_right(k):
+        return remote(raw[k].at[..., pl.ds(cols - LANES, LANES)], ext[k].at[..., pl.ds(0, LANES)],
+                      col_ss.at[k, 0], col_rs.at[k, 0], lev=ml + 1)
+
+    def col_left(k):
+        return remote(raw[k].at[..., pl.ds(0, LANES)], ext[k].at[..., pl.ds(LANES + cols, LANES)],
+                      col_ss.at[k, 1], col_rs.at[k, 1], lev=ml - 1)
+
+    @pl.when(ml < Q - 1)
+    def _():
+        for k in (0, 5, 1, 2, 3, 4):
+            col_right(k).start()
+
+    @pl.when(ml > 0)
+    def _():
+        for k in (0, 5, 1, 2, 3, 4):
+            col_left(k).start()
+
+    def col_wait(ks):
+        @pl.when(ml > 0)
+        def _():
+            for k in ks:
+                col_right(k).wait_recv()
+
+        @pl.when(ml < Q - 1)
+        def _():
+            for k in ks:
+                col_left(k).wait_recv()
+
+    whole_c, low_c, high_c = pl.ds(LANES, cols), pl.ds(0, LANES), pl.ds(LANES + cols, LANES)
+    first_c, last_c, every_c = pl.ds(0, LANES), pl.ds(cols - LANES, LANES), pl.ds(0, cols)
+    moves = (
+        (vsu, vrb, -1, 0, every_c, whole_c), (vsu, vrb, -1, -1, first_c, high_c), (vsu, vrb, -1, 1, last_c, low_c),
+        (vsd, vrt, 1, 0, every_c, whole_c), (vsd, vrt, 1, -1, first_c, high_c), (vsd, vrt, 1, 1, last_c, low_c),
+    )
+
+    def there(i, j, sign):
+        ok = mt > 0 if i * sign < 0 else mt < T - 1
+        if j == 0:
+            return ok
+        return jnp.logical_and(ok, ml > 0 if j * sign < 0 else ml < Q - 1)
+
+    def v_move(n):
+        src, dst, i, j, sc, dc = moves[n]
+        return remote(src.at[:, sc], dst.at[:, dc], v_ss.at[n], v_rs.at[n], tiles=mt + i, lev=ml + j)
+
+    for n in range(6):
+        @pl.when(there(moves[n][2], moves[n][3], 1))
+        def _():
+            v_move(n).start()
+
+    @pl.when(ml == 0)
+    def _():
+        vrt[:, 0:LANES] = jnp.zeros((2 * levels + 1, LANES), F32)
+        vrb[:, 0:LANES] = jnp.zeros((2 * levels + 1, LANES), F32)
+
+    @pl.when(ml == Q - 1)
+    def _():
+        vrt[:, LANES + cols:] = jnp.zeros((2 * levels + 1, LANES), F32)
+        vrb[:, LANES + cols:] = jnp.zeros((2 * levels + 1, LANES), F32)
 
     acc = jnp.zeros((nslot, cells), F32)
     for c in range(nchunk):
@@ -181,22 +206,9 @@
         payload[t, :, 0:cells] = acc[t * cap:(t + 1) * cap, :]
         payload[t, :, cells:] = ids[t * cap:(t + 1) * cap, :]
 
-    col_wait((1, 2, 3, 4))
-
-    @pl.when(mt < T - 1)
-    def _():
-        v_up().wait_recv()
-
-    @pl.when(mt > 0)
-    def _():
-        v_down().wait_recv()
-
     def a2a(d):
         to = lax.rem(mt + d, T)
         return remote(payload.at[to], rec.at[d - 1], a_ss.at[d - 1], a_rs.at[d - 1], tiles=to)
-
-    for d in range(1, T):
-        a2a(d).start()
 
     row_id = lax.broadcasted_iota(jnp.int32, (rows, wide), 0)
 
@@ -211,31 +223,62 @@
         q = VISC_FLOOR + 0.25 * (dx * dx) + 0.25 * (dy * dy)
         return fr * (root * jnp.exp(jnp.log(q) * (-1.0 / 6.0)))
 
+    def across(x):
+        return pltpu.roll(x, wide - 1, 1) - pltpu.roll(x, 1, 1)
+
+    col_wait((0, 5))
+    frac = mask_e[...].astype(F32)
+
+    def s_level(l, carry):
+        x = v_e[l]
+        s_f[l + 1] = s_from(pltpu.roll(x, rows - 1, 0) - pltpu.roll(x, 1, 0), across(x), frac)
+        o_t[pl.ds(l, 1), :] = x[0:1, :]
+        i_t[pl.ds(l, 1), :] = x[1:2, :]
+        i_b[pl.ds(l, 1), :] = x[rows - 2:rows - 1, :]
+        o_b[pl.ds(l, 1), :] = x[rows - 1:rows, :]
+        return carry
+
+    lax.fori_loop(0, levels, s_level, 0)
+    load_wait((1, 2, 3, 4))
+    col_wait((1, 2, 3, 4))
+    drag = frac * fric_e[...] + (1.0 - frac)
+    drag_s = drag * inv_sigma - 1.0
+    coef = frac * (thk_e[...] + SMB_WEIGHT * prev_e[...])
+
+    for n in range(6):
+        @pl.when(there(moves[n][2], moves[n][3], -1))
+        def _():
+            v_move(n).wait_recv()
+
     near_t, far_t = vrt[0:levels, :], vrt[levels:2 * levels, :]
     near_b, far_b = vrb[0:levels, :], vrb[levels:2 * levels, :]
-    own_t, own_b = vsu[0:levels, :], vsd[0:levels, :]
-    sht[...] = s_from(own_t - far_t, pltpu.roll(near_t, wide - 1, 1) - pltpu.roll(near_t, 1, 1),
-                      vrt[2 * levels:2 * levels + 1, :])
-    shb[...] = s_from(far_b - own_b, pltpu.roll(near_b, wide - 1, 1) - pltpu.roll(near_b, 1, 1),
-                      vrb[2 * levels:2 * levels + 1, :])
-
-    def s_level(l, carry):
-        x = v_e[l]
-        before, after, low, high = around(x, vrt[pl.ds(l, 1), :], vrb[pl.ds(l, 1), :])
-        s = s_from(after - before, high - low, frac)
+    own_t, own_b = o_t[...], o_b[...]
+    sht[...] = s_from(own_t - far_t, across(near_t), vrt[2 * levels:2 * levels + 1, :])
+    shb[...] = s_from(far_b - own_b, across(near_b), vrb[2 * levels:2 * levels + 1, :])
+    se_t[...] = s_from(i_t[...] - near_t, across(own_t), frac[0:1, :])
+    se_b[...] = s_from(near_b - i_b[...], across(own_b), frac[rows - 1:rows, :])
+
+    def with_edges(x, top, bot):
+        return jnp.where(row_id == 0, top, jnp.where(row_id == rows - 1, bot, x))
+
+    def fix_level(l, carry):
+        s = with_edges(s_f[l + 1], se_t[pl.ds(l, 1), :], se_b[pl.ds(l, 1), :])
         s_f[l + 1] = s
-        w_f[l + 1] = s * x
+        w_f[l + 1] = s * v_e[l]
         return carry
 
-    lax.fori_loop(0, levels, s_level, 0)
+    lax.fori_loop(0, levels, fix_level, 0)
 
     def total(ref, l, top, bot):
         before, after, low, high = around(ref[l + 1], top, bot)
         return ((before + after) + (low + high)) + VERTICAL * (ref[l] + ref[l + 2])
 
-    drag = frac * fric_e[...] + (1.0 - frac)
-    drag_s = drag * inv_sigma - 1.0
-    coef = frac * (thk_e[...] + SMB_WEIGHT * prev_e[...])
+    def inside(l):
+        x = w_f[l + 1]
+        after = jnp.where(row_id == rows - 1, 0.0, pltpu.roll(x, rows - 1, 0))
+        before = jnp.where(row_id == 0, 0.0, pltpu.roll(x, 1, 0))
+        sides = pltpu.roll(x, 1, 1) + pltpu.roll(x, wide - 1, 1)
+        return ((before + after) + sides) + VERTICAL * (w_f[l] + w_f[l + 2])
 
     def start_level(l, carry):
         st, sb = sht[pl.ds(l, 1), :], shb[pl.ds(l, 1), :]
@@ -249,6 +292,8 @@
         w = s * r
         su[0, pl.ds(l, 1), :] = w[0:1, :]
         sd[0, pl.ds(l, 1), :] = w[rows - 1:rows, :]
+        ve_t[pl.ds(l, 1), :] = r[0:1, :]
+        ve_b[pl.ds(l, 1), :] = r[rows - 1:rows, :]
         return carry
 
     lax.fori_loop(0, levels, start_level, 0)
@@ -260,18 +305,20 @@
         return remote(sd.at[k], rt.at[k], row_ss.at[k, 1], row_rs.at[k, 1], tiles=mt + 1)
 
     def row_start(k):
-        @pl.when(mt > 0)
-        def _():
-            row_up(k).start()
+        if k + 1 < ITERS:
+            @pl.when(mt > 0)
+            def _():
+                row_up(k).start()
 
         @pl.when(mt < T - 1)
         def _():
             row_down(k).start()
 
     def row_wait(k):
-        @pl.when(mt < T - 1)
-        def _():
-            row_up(k).wait_recv()
+        if k + 1 < ITERS:
+            @pl.when(mt < T - 1)
+            def _():
+                row_up(k).wait_recv()
 
         @pl.when(mt > 0)
         def _():
@@ -307,46 +354,69 @@
         for d in range(1, Q):
             gather(d, ml).start()
 
-    own = slice(LANES, LANES + cols)
-
-    def fold(x):
-        return jnp.sum(x[:, own], axis=0, keepdims=True)
-
+    def put(j, value):
+        line = jnp.sum(value, axis=0, keepdims=True)
+        piece = line[:, 0:LANES]
+        for i in range(1, cols // LANES):
+            piece = piece + line[:, i * LANES:(i + 1) * LANES]
+        g_send[j:j + 1, :] = piece
+
+    zero = jnp.zeros((rows, cols), F32)
+    half = T // 2
     for k in range(ITERS):
         row_start(k)
-
-        def w_level(l, carry):
-            w_f[l + 1] = s_f[l + 1] * k_f[k, l]
+        if k == 0:
+            for d in range(1, half):
+                a2a(d).start()
+        if k == 1:
+            for d in range(half, T):
+                a2a(d).start()
+
+        def fill_level(l, carry):
+            v = k_f[k, l]
+            if k > 0:
+                v = with_edges(v, ve_t[pl.ds(l, 1), :], ve_b[pl.ds(l, 1), :])
+                k_f[k, l] = v
+            w_f[l + 1] = s_f[l + 1] * v
+            mine = v[:, own]
+            if k == 0:
+                return carry[0] + mine * mine, carry[1]
+            return carry[0] + mine * mine, carry[1] + k_f[k - 1, l][:, own] * mine
+
+        now, cross = lax.fori_loop(0, levels, fill_level, (zero, zero))
+        put(2 * k, now)
+        if k > 0:
+            put(2 * k - 1, cross)
+
+        def part_level(l, carry):
+            v = k_f[k, l]
+            nxt = d_f[l] * v - s_f[l + 1] * inside(l)
+            if k + 1 == ITERS:
+                return carry + v[:, own] * nxt[:, own]
+            k_f[k + 1, l] = nxt
+            pe_t[pl.ds(l, 1), :] = nxt[0:1, :]
+            pe_b[pl.ds(l, 1), :] = nxt[rows - 1:rows, :]
             return carry
 
-        lax.fori_loop(0, levels, w_level, 0)
-        if k == 1:
+        if k + 1 == ITERS:
+            last = lax.fori_loop(0, levels, part_level, zero)
+        else:
+            lax.fori_loop(0, levels, part_level, 0)
+        if k == 2:
             tile_sums()
         if k == 3:
             lev_sums()
         row_wait(k)
-
-        def step_level(l, carry):
-            now, cross = carry
-            s = s_f[l + 1]
-            v = k_f[k, l]
-            nxt = d_f[l] * v - s * total(w_f, l, rt[k, pl.ds(l, 1), :], rb[k, pl.ds(l, 1), :])
-            if k + 1 < ITERS:
-                k_f[k + 1, l] = nxt
-                w = s * nxt
-                su[k + 1, pl.ds(l, 1), :] = w[0:1, :]
-                sd[k + 1, pl.ds(l, 1), :] = w[rows - 1:rows, :]
-            v, nxt = v[:, own], nxt[:, own]
-            return now + v * v, cross + v * nxt
-
-        zero = jnp.zeros((rows, cols), F32)
-        now, cross = lax.fori_loop(0, levels, step_level, (zero, zero))
-        for j, value in ((2 * k, now), (2 * k + 1, cross)):
-            line = jnp.sum(value, axis=0, keepdims=True)
-            piece = line[:, 0:LANES]
-            for i in range(1, cols // LANES):
-                piece = piece + line[:, i * LANES:(i + 1) * LANES]
-            g_send[j:j + 1, :] = piece
+        if k + 1 < ITERS:
+            top = pe_t[...] - se_t[...] * rt[k]
+            bot = pe_b[...] - se_b[...] * rb[k]
+            ve_t[...] = top
+            ve_b[...] = bot
+            su[k + 1] = se_t[...] * top
+            sd[k + 1] = se_b[...] * bot
+        else:
+            pairs = jnp.sum(su[k][:, own] * rt[k][:, own], axis=0, keepdims=True)
+            put(2 * k + 1, jnp.where(row_id[:, own] == 0, last - 2.0 * pairs, last))
 
     def g_lev_copy(d):
         return remote(g_send, g_lev.at[d - 1], gl_ss.at[d - 1], gl_rs.at[d - 1], lev=lax.rem(ml + d, Q))
@@ -365,7 +435,12 @@
         g_til_copy(d).start()
     for d in range(1, Q):
         gather(d, lax.rem(ml - d + Q, Q)).wait_recv()
-    tot_out[...] = tot_s[...]
+    share_l = tot_s.shape[2] // LANES
+    for q in range(Q):
+        for i in range(share_l):
+            for t in range(tpd):
+                tot_out[q * share_l + i:q * share_l + i + 1, t * LANES:(t + 1) * LANES] = (
+                    tot_s[q, t:t + 1, i * LANES:(i + 1) * LANES])
     for d in range(1, T):
         g_til_copy(d).wait_recv()
         value = value + g_til[d - 1]
@@ -422,15 +497,18 @@
         for k in range(6):
             col_left(k).wait_send()
 
+    for n in range(6):
+        @pl.when(there(moves[n][2], moves[n][3], 1))
+        def _():
+            v_move(n).wait_send()
+
     @pl.when(mt > 0)
     def _():
-        v_up().wait_send()
-        for k in range(ITERS):
+        for k in range(ITERS - 1):
             row_up(k).wait_send()
 
     @pl.when(mt < T - 1)
     def _():
-        v_down().wait_send()
         for k in range(ITERS):
             row_down(k).wait_send()
 
@@ -451,8 +529,7 @@
     tpd = cols * Q // LANES
     cap = max(2, 2 * nblk // T)
     cap = -(-cap // 8) * 8
-    stride = -(-land_smb.shape[1] // 16) * 16
-    lrows = -(-land_smb.shape[0] * stride // LANES) * LANES
+    lrows = -(-land_smb.shape[0] * land_smb.shape[1] // LANES) * LANES
     share = cells // Q
     dma = pltpu.SemaphoreType.DMA
     vm = pl.BlockSpec(memory_space=pltpu.VMEM)
@@ -462,9 +539,9 @@
     def f(*shape):
         return pltpu.VMEM(shape, F32)
 
-    totals, velocity = pl.pallas_call(
+    return pl.pallas_call(
         functools.partial(kernel, T, Q, cap, tpd),
-        out_shape=(jax.ShapeDtypeStruct((Q, tpd, share), F32),
+        out_shape=(jax.ShapeDtypeStruct((rows, tpd * LANES), F32),
                    jax.ShapeDtypeStruct(velocity_start.shape, F32)),
         in_specs=[vm, anyw, sm, sm, sm] + [anyw] * 6,
         out_specs=(vm, vm),
@@ -473,27 +550,25 @@
             pltpu.VMEM((rows, wide), jnp.int32),
             f(levels + 2, rows, wide), f(levels, rows, wide), f(levels + 2, rows, wide),
             f(ITERS, levels, rows, wide),
-            f(2 * levels + 1, wide), f(2 * levels + 1, wide), f(2 * levels + 1, wide), f(2 * levels + 1, wide),
+            f(2 * levels + 1, cols), f(2 * levels + 1, cols), f(2 * levels + 1, wide), f(2 * levels + 1, wide),
             f(ITERS, levels, wide), f(ITERS, levels, wide), f(ITERS, levels, wide), f(ITERS, levels, wide),
             f(levels, wide), f(levels, wide),
-            f(8, LANES), f(2 * ITERS, LANES), f(Q - 1, 2 * ITERS, LANES), f(2 * ITERS, LANES),
+            *[f(levels, wide) for _ in range(10)],
+            f(2 * ITERS, LANES), f(Q - 1, 2 * ITERS, LANES), f(2 * ITERS, LANES),
             f(T - 1, 2 * ITERS, LANES),
             pltpu.VMEM(block_weights.shape, block_weights.dtype),
             f(lrows, LANES), pltpu.VMEM((nblk, lrows), jnp.int32), pltpu.VMEM((nblk, LANES), jnp.int32),
             f(T, cap, cells + LANES), f(T, cap, cells + LANES),
             f(Q, tpd, share), f(Q - 1, tpd, share), f(Q, tpd, share),
-            dma((6,)), dma((4,)), dma((6, 2)), dma((6, 2)), dma((ITERS, 2)), dma((ITERS, 2)), dma((2,)), dma((2,)),
+            dma((6,)), dma((4,)), dma((6, 2)), dma((6, 2)), dma((ITERS, 2)), dma((ITERS, 2)), dma((6,)), dma((6,)),
             dma((Q - 1,)), dma((Q - 1,)), dma((T - 1,)), dma((T - 1,)), dma((T - 1,)), dma((T - 1,)),
             dma((Q - 1,)), dma((Q - 1,)), dma((Q - 1,)), dma((Q - 1,)),
         ],
         compiler_params=pltpu.CompilerParams(collective_id=0, has_side_effects=True,
                                              vmem_limit_bytes=60 * 1024 * 1024),
         name="remap_and_solve",
-    )(land_smb, block_weights, block_tile, block_land, block_class, ice_mask, thickness, prev_smb,
+    )(land_smb.transpose(1, 0, 2), block_weights, block_tile, block_land, block_class, ice_mask, thickness, prev_smb,
       basal_friction, driving, velocity_start)
-    per = share // LANES
-    ice_smb = totals.reshape(Q, tpd, per, LANES).transpose(0, 2, 1, 3).reshape(rows, tpd * LANES)
-    return ice_smb, velocity
 
 
 def solution(mesh):

time: 57.3 us -> 49.8 us (0.87)
  Pallas kernels: 51.5 us -> 45.7 us
  local copies, waits for them, and re-layouts: 4.86 us -> 3.29 us
    pallas_call x1, Pallas kernels: 51.5 us -> 45.7 us  [body(): pl.pallas_call(functools.partial(kernel, T, Q, cap, tpd), out_shape=(jax....]
    reshape x1 -> x0, local copies, waits for them, and re-layouts: 0.97 us -> none  [body(): totals.reshape(Q, tpd, per, LANES).transpose(0, 2, 1, 3)]
    unnamed x3 -> x2, local copies, waits for them, and re-layouts: 3.88 us -> 3.29 us
where the time goes in v2:
time: 49.8 us; the launch traced here: 49.6 us
  Pallas kernels  45.7 us (92%)
  local copies, waits for them, and re-layouts  3.29 us (7%)
  between operations  0.64 us (1%)
    pallas_call x1, Pallas kernels, body(): pl.pallas_call(functools.partial(kernel, T, Q, cap, tpd), out_shape=(jax....  45.7 us
    unnamed x2, local copies, waits for them, and re-layouts  3.29 us

profile of v2, /device:TPU:0, one launch (start us, length us, event | category | flops | bytes accessed | tf_op | source)
XLA Modules:
  0.0 49.6 jit_solution(2018418181771217981)
XLA Ops:
  0.6 45.7 %remap_and_solve.1 = (f32[8,4096]{1,0:T(8,128)}, f32[10,8,1024]{2,1,0:T(8,128)}) custom-call(bf16[10,16,128]{2,1,0:T(8,128)(2,1)} %bitcast.1, bf16[32,128,1024]{2,1,0:T(8,128)(2,1)} %wts.1, s32[32]{0:T(128)} %btile.1, s32[32]{0:T(128)} %bland.1, s32[32]{0:T(128)} %bclass.1, s32[8,1024]{1,0:T(8,128)} %mask.1, f32[8,1024]{1,0:T(8,128)} %thk.1, ...), custom_call_target="tpu_custom_call" | custom-call | tf_op jit(solution)/shard_map/remap_and_solve/pallas_call | solution.py:542
  46.3 1.6 %copy.15 = f32[8,4096]{1,0:T(8,128)} copy(f32[8,4096]{1,0:T(8,128)} %get-tuple-element.4) | data formatting | bytes 262144
  47.9 1.7 %copy.16 = f32[10,8,1024]{2,1,0:T(8,128)} copy(f32[10,8,1024]{2,1,0:T(8,128)} %get-tuple-element.5) | data formatting | bytes 655360

commit v3 on v2

--- a/solution.py
+++ b/solution.py
@@ -521,6 +521,25 @@
         g_lev_copy(d).wait_send()
 
 
+def hand_out(smb, velocity):
+    def both(a, b, a_out, b_out, sem):
+        first = pltpu.make_async_copy(a, a_out, sem.at[0])
+        second = pltpu.make_async_copy(b, b_out, sem.at[1])
+        first.start()
+        second.start()
+        first.wait()
+        second.wait()
+
+    return pl.pallas_call(
+        both,
+        out_shape=(jax.ShapeDtypeStruct(smb.shape, F32), jax.ShapeDtypeStruct(velocity.shape, F32)),
+        in_specs=[pl.BlockSpec(memory_space=pltpu.VMEM)] * 2,
+        out_specs=(pl.BlockSpec(memory_space=pl.ANY),) * 2,
+        scratch_shapes=[pltpu.SemaphoreType.DMA((2,))],
+        name="hand_out",
+    )(smb, velocity)
+
+
 def body(T, Q, land_smb, block_weights, block_tile, block_land, block_class, ice_mask,
          thickness, prev_smb, basal_friction, driving, velocity_start):
     levels, rows, cols = velocity_start.shape
@@ -539,7 +558,7 @@
     def f(*shape):
         return pltpu.VMEM(shape, F32)
 
-    return pl.pallas_call(
+    totals, velocity = pl.pallas_call(
         functools.partial(kernel, T, Q, cap, tpd),
         out_shape=(jax.ShapeDtypeStruct((rows, tpd * LANES), F32),
                    jax.ShapeDtypeStruct(velocity_start.shape, F32)),
@@ -569,6 +588,7 @@
         name="remap_and_solve",
     )(land_smb.transpose(1, 0, 2), block_weights, block_tile, block_land, block_class, ice_mask, thickness, prev_smb,
       basal_friction, driving, velocity_start)
+    return hand_out(totals, velocity)
 
 
 def solution(mesh):

time: 49.8 us -> 48.3 us (0.970)
  local copies, waits for them, and re-layouts: 3.29 us -> 0 us
  Pallas kernels: 45.7 us -> 47.5 us
    unnamed x2 -> x0, local copies, waits for them, and re-layouts: 3.29 us -> none
    pallas_call x0 -> x1, Pallas kernels: none -> 1.83 us  [hand_out(): pl.pallas_call(both, out_shape=(jax.ShapeDtypeStruct(smb.shape, F32), jax...]
where the time goes in v3:
time: 48.3 us; the launch traced here: 48.1 us
  Pallas kernels  47.5 us (98%)
  between operations  0.64 us (1%)
    pallas_call x1, Pallas kernels, body(): pl.pallas_call(functools.partial(kernel, T, Q, cap, tpd), out_shape=(jax....  45.7 us
    pallas_call x1, Pallas kernels, hand_out(): pl.pallas_call(both, out_shape=(jax.ShapeDtypeStruct(smb.shape, F32), jax...  1.83 us

profile of v3, /device:TPU:0, one launch (start us, length us, event | category | flops | bytes accessed | tf_op | source)
XLA Modules:
  0.0 48.1 jit_solution(443145605157592690)
XLA Ops:
  0.6 45.7 %remap_and_solve.1 = (f32[8,4096]{1,0:T(8,128)}, f32[10,8,1024]{2,1,0:T(8,128)}) custom-call(bf16[10,16,128]{2,1,0:T(8,128)(2,1)} %bitcast.1, bf16[32,128,1024]{2,1,0:T(8,128)(2,1)} %wts.1, s32[32]{0:T(128)} %btile.1, s32[32]{0:T(128)} %bland.1, s32[32]{0:T(128)} %bclass.1, s32[8,1024]{1,0:T(8,128)} %mask.1, f32[8,1024]{1,0:T(8,128)} %thk.1, ...), custom_call_target="tpu_custom_call" | custom-call | tf_op jit(solution)/shard_map/remap_and_solve/pallas_call | solution.py:561
  46.3 1.8 %hand_out.1 = (f32[8,4096]{1,0:T(8,128)}, f32[10,8,1024]{2,1,0:T(8,128)}) custom-call(f32[8,4096]{1,0:T(8,128)} %get-tuple-element.4.a, f32[10,8,1024]{2,1,0:T(8,128)} %get-tuple-element.5.b), custom_call_target="tpu_custom_call" | custom-call | tf_op jit(solution)/shard_map/hand_out/pallas_call | solution.py:533
